TPU v7x, 256 devices: a whole 4x4x8 slice. The times are simulated.
256 devices in a mesh: row: 16 (over z, core), col: 16 (over x, y).
Axes of the slice: x: 4, y: 4, z: 8, core: 2. Of those that a mesh axis runs over, the one named last changes fastest.
Arguments:
- matrix: bfloat16 [7, 4096, 7, 4096], P(None, 'row', None, 'col'), may hold values from -1 to 3
- pivots: int32 [2, 256], replicated, may hold values from 256 to 28671, as said below
Outputs:
- factored: bfloat16 [7, 4096, 7, 4096], P(None, 'row', None, 'col')
Inputs may be any that keep to these rules, and one draw needn't show every extreme that they name: Within a step s the pivots[s, :] are distinct and lie in (s + 1) * 256 to 28671.
All inputs are finite; a program needn't handle non-finite values.
Results may differ from a plain program's by a relative error of at most 0.0059.
Values may be sent and summed in bfloat16 or wider, within the bound.
A program may use at most 64 MiB of HBM per device.

v0:
```python
import jax
import jax.numpy as jnp
from jax import lax
from jax.sharding import PartitionSpec as P

STEPS = 2
NEWTON = 3


def broadcast(shard, axis, root):
    mine = lax.axis_index(axis) == root
    return lax.psum(jnp.where(mine, shard, jnp.zeros_like(shard)), axis)


def newton_inverse(diag_block):
    identity = jnp.eye(diag_block.shape[0], dtype=jnp.float32)
    approx = identity / 3.0
    for _ in range(NEWTON):
        product = jnp.dot(diag_block, approx, precision=lax.Precision.HIGHEST)
        approx = jnp.dot(approx, 2.0 * identity - product, precision=lax.Precision.HIGHEST)
    return approx


def body(matrix, pivots):
    row_count = lax.axis_size("row")
    col_count = lax.axis_size("col")
    row_index = lax.axis_index("row")
    col_index = lax.axis_index("col")
    row_cycles, block_size, col_cycles, _ = matrix.shape
    local_rows = row_cycles * block_size
    local_cols = col_cycles * block_size
    current = matrix.reshape(local_rows, local_cols)
    row_positions = jnp.arange(local_rows, dtype=jnp.int32)
    col_positions = jnp.arange(local_cols, dtype=jnp.int32)
    global_row = (
        row_positions // block_size * row_count * block_size
        + row_index * block_size
        + row_positions % block_size
    )
    global_col = (
        col_positions // block_size * col_count * block_size
        + col_index * block_size
        + col_positions % block_size
    )
    identity = jnp.eye(block_size, dtype=jnp.float32)
    for panel_step in range(STEPS):
        after_row = (panel_step + 1) * block_size
        owner_row = panel_step % row_count
        owner_cycle = panel_step // row_count
        owner_col = panel_step % col_count
        panel_cycle = panel_step // col_count
        chosen = pivots[panel_step]
        owner_of = chosen // block_size % row_count
        local_at = chosen // (block_size * row_count) * block_size + chosen % block_size
        is_mine = owner_of == row_index
        picked = jnp.where(
            is_mine[:, None],
            current[jnp.clip(local_at, 0, local_rows - 1)],
            jnp.zeros((), jnp.bfloat16),
        )
        top_rows = current[owner_cycle * block_size : (owner_cycle + 1) * block_size]
        is_top = row_index == owner_row
        new_top = lax.psum(picked, "row").astype(jnp.float32).astype(jnp.bfloat16)
        old_top = broadcast(top_rows, "row", owner_row)
        target = jnp.where(is_mine, local_at, local_rows)
        current = current.at[target].set(old_top, mode="drop")
        kept_rows = current[owner_cycle * block_size : (owner_cycle + 1) * block_size]
        current = current.at[owner_cycle * block_size : (owner_cycle + 1) * block_size].set(
            jnp.where(is_top, new_top, kept_rows)
        )
        panel_block = current[:, panel_cycle * block_size : (panel_cycle + 1) * block_size]
        is_owner = col_index == owner_col
        diag_block = jnp.where(
            is_owner,
            new_top[:, panel_cycle * block_size : (panel_cycle + 1) * block_size].astype(
                jnp.float32
            ),
            3.0 * identity,
        )
        below_mask = (global_row >= after_row)[:, None]
        inverse = newton_inverse(diag_block)
        own_lower = jnp.where(
            below_mask,
            jnp.dot(panel_block.astype(jnp.float32), inverse, precision=lax.Precision.HIGHEST),
            0.0,
        ).astype(jnp.bfloat16)
        lower_panel = broadcast(own_lower, "col", owner_col)
        right_mask = (global_col >= after_row)[None, :]
        upper_rows = jnp.where(right_mask, new_top, jnp.zeros_like(new_top))
        change = jnp.dot(lower_panel, upper_rows, preferred_element_type=jnp.float32)
        current = (current.astype(jnp.float32) - change).astype(jnp.bfloat16)
        old_panel = current[:, panel_cycle * block_size : (panel_cycle + 1) * block_size]
        current = current.at[:, panel_cycle * block_size : (panel_cycle + 1) * block_size].set(
            jnp.where(jnp.logical_and(is_owner, below_mask), lower_panel, old_panel)
        )
    return current.reshape(row_cycles, block_size, col_cycles, block_size)


def solution(mesh):
    return jax.shard_map(
        body,
        mesh=mesh,
        in_specs=(P(None, "row", None, "col"), P()),
        out_specs=P(None, "row", None, "col"),
        check_vma=False,
    )
```

profile of v0, /device:TPU:32, one launch (start us, length us, event | category | flops | bytes accessed | tf_op | source)
XLA Modules:
  0.0 546.3 jit_solution(16321497234872604605)
XLA Ops:
  6.5 0.0 all-reduce.13.cloned.1.call-start
  6.5 6.8 %copy.6 = bf16[7,256,7,256]{3,2,1,0:T(8,128)(2,1)S(1)} copy(bf16[7,256,7,256]{3,1,2,0:T(8,128)(2,1)} %param.10) | data formatting | bytes 12845056 | tf_op args[0]
  13.4 0.0 copy-done.4
  13.4 0.0 slice-start
  13.4 5.6 %copy.11 = bf16[224,8,7,256]{3,1,2,0:T(8,128)(2,1)} copy(bf16[224,8,7,256]{3,2,1,0:T(8,128)(2,1)S(1)} %bitcast.68) | data formatting | bytes 12845056
  19.0 0.6 copy.10
  19.7 0.1 broadcast_select_fusion.2
  19.7 1.4 copy.8
  21.2 5.8 %gather_fusion = bf16[256,1792]{1,0:T(8,128)(2,1)S(1)} fusion(bf16[1792,1792]{1,0:T(8,128)(2,1)} %bitcast.66, s32[1024]{0:T(1024)S(1)} %pad_clamp_fusion.1), kind=kCustom, calls=%fused_computation | custom fusion | bytes 1836032 | tf_op jit(solution)/shard_map/gather | solution.py:58
  27.0 1.1 broadcast_select_fusion.1
  28.0 0.0 all-reduce.13.cloned.1.call-update
  28.1 0.5 all-reduce.7.cloned.1.call-start
  28.6 114.3 %all-reduce.13.cloned.1.call-done = (bf16[256,1792]{1,0:T(8,128)(2,1)}, bf16[256,1792]{1,0:T(8,128)(2,1)}) async-done(((bf16[256,1792]{1,0:T(8,128)(2,1)}, bf16[256,1792]{1,0:T(8,128)(2,1)}), (bf16[256,1792]{1,0:T(8,128)(2,1)}, bf16[256,1792]{1,0:T(8,128)(2,1)})) %all-reduce.13.cloned.1.call-update) | async-done | bytes 1835024 | tf_op jit(solution)/shard_map/psum | solution.py:12
  142.9 9.5 %scatter_fusion = bf16[1792,1792]{1,0:T(8,128)(2,1)} fusion(bf16[1792,1792]{1,0:T(8,128)(2,1)} %bitcast.67, s32[256]{0:T(256)S(1)} %bitcast.70, bf16[256,1792]{1,0:T(8,128)(2,1)} %get-tuple-element.55), kind=kCustom, calls=%fused_computation.2 | custom fusion | bytes 2753536 | tf_op jit(solution)/shard_map/scatter | solution.py:66
  152.4 2.3 fusion.9
  154.7 0.4 convolution_subtract_fusion.5
  155.1 0.4 fusion.17
  155.5 0.4 convolution_subtract_fusion.4
  155.9 0.4 fusion.99
  156.3 0.4 convolution_subtract_fusion.3
  156.7 0.4 fusion.100
  157.1 3.1 fusion.3
  160.2 0.0 all-reduce.7.cloned.1.call-update
  160.2 0.2 all-reduce.11.cloned.1.call-start
  160.4 0.6 compare_reduce_fusion
  161.1 98.7 %all-reduce.7.cloned.1.call-done = bf16[1792,256]{1,0:T(8,128)(2,1)} async-done(((bf16[1792,256]{1,0:T(8,128)(2,1)}), bf16[1792,256]{1,0:T(8,128)(2,1)}) %all-reduce.7.cloned.1.call-update) | async-done | bytes 917520 | tf_op jit(solution)/shard_map/psum | solution.py:12
  259.9 7.8 %subtract_convert_fusion.1 = bf16[1792,1792]{1,0:T(8,128)(2,1)} fusion(bf16[1792,1792]{1,0:T(8,128)(2,1)} %fusion.9, bf16[1792,256]{1,0:T(8,128)(2,1)} %all-reduce.7.cloned.1.call-done, bf16[256,1792]{1,0:T(8,128)(2,1)S(1)} %copy-done.2, pred[1792]{0:T(1024)(128)(4,1)S(1)} %fusion.67), kind=kOutput, calls=%fused_computation.5 | convolution fusion | flops 1654259712 | bytes 14681856 | tf_op jit(solution)/shard_map/dot_general | solution.py:90
  267.6 3.3 fusion.4
  270.9 5.8 %gather_fusion.1 = bf16[256,1792]{1,0:T(8,128)(2,1)S(1)} fusion(bf16[1792,1792]{1,0:T(8,128)(2,1)} %fusion.4, s32[1024]{0:T(1024)S(1)} %pad_clamp_fusion), kind=kCustom, calls=%fused_computation.1 | custom fusion | bytes 1836032 | tf_op jit(solution)/shard_map/gather | solution.py:58
  276.7 2.6 slice_select_fusion.1
  279.4 0.0 all-reduce.11.cloned.1.call-update
  279.4 0.0 all-reduce.9.cloned.1.call-start
  279.5 111.2 %all-reduce.11.cloned.1.call-done = (bf16[256,1792]{1,0:T(8,128)(2,1)}, bf16[256,1792]{1,0:T(8,128)(2,1)}) async-done(((bf16[256,1792]{1,0:T(8,128)(2,1)}, bf16[256,1792]{1,0:T(8,128)(2,1)}), (bf16[256,1792]{1,0:T(8,128)(2,1)}, bf16[256,1792]{1,0:T(8,128)(2,1)})) %all-reduce.11.cloned.1.call-update) | async-done | bytes 1835024 | tf_op jit(solution)/shard_map/psum | solution.py:12
  390.7 9.7 %scatter_fusion.1 = bf16[1792,1792]{1,0:T(8,128)(2,1)} fusion(bf16[1792,1792]{1,0:T(8,128)(2,1)} %fusion.4, s32[256]{0:T(256)S(1)} %bitcast.71, bf16[256,1792]{1,0:T(8,128)(2,1)} %get-tuple-element.53), kind=kCustom, calls=%fused_computation.3 | custom fusion | bytes 2753536 | tf_op jit(solution)/shard_map/scatter | solution.py:66
  400.4 2.3 fusion.7
  402.7 0.4 convolution_subtract_fusion.2
  403.1 0.4 fusion.14
  403.5 0.4 convolution_subtract_fusion.1
  403.9 0.4 fusion.101
  404.3 0.4 convolution_subtract_fusion
  404.7 0.4 fusion.102
  405.1 3.1 fusion.2
  408.2 0.0 all-reduce.9.cloned.1.call-update
  408.2 99.6 %all-reduce.9.cloned.1.call-done = bf16[1792,256]{1,0:T(8,128)(2,1)} async-done(((bf16[1792,256]{1,0:T(8,128)(2,1)}), bf16[1792,256]{1,0:T(8,128)(2,1)}) %all-reduce.9.cloned.1.call-update) | async-done | bytes 917520 | tf_op jit(solution)/shard_map/psum | solution.py:12
  507.9 7.8 %subtract_convert_fusion = bf16[1792,1792]{1,0:T(8,128)(2,1)} fusion(bf16[1792,1792]{1,0:T(8,128)(2,1)} %fusion.7, bf16[1792,256]{1,0:T(8,128)(2,1)} %all-reduce.9.cloned.1.call-done, bf16[256,1792]{1,0:T(8,128)(2,1)S(1)} %copy-done.3, pred[1792]{0:T(1024)(128)(4,1)S(1)} %fusion.66), kind=kOutput, calls=%fused_computation.4 | convolution fusion | flops 1654259712 | bytes 14681856 | tf_op jit(solution)/shard_map/dot_general | solution.py:90
  515.6 3.3 fusion.5
  518.9 13.0 %reshape.600 = bf16[7,256,7,256]{3,2,1,0:T(8,128)(2,1)} reshape(bf16[1792,1792]{1,0:T(8,128)(2,1)} %fusion.5) | data formatting | bytes 12845056 | tf_op jit(solution)/shard_map/reshape | solution.py:96
  532.0 7.6 %copy.9 = bf16[7,256,7,256]{3,1,2,0:T(8,128)(2,1)} copy(bf16[7,256,7,256]{3,2,1,0:T(8,128)(2,1)} %reshape.600) | data formatting | bytes 12845056 | tf_op jit(solution)/shard_map/reshape | solution.py:96
  (24 shorter events, 0.2 us)
Async XLA Ops:
  6.5 136.4 %all-reduce.13.cloned.1.call-start = ((), (), s32[]{:S(2)}) async-start(), calls=%async_computation.3 | async-start | bytes 3670016 | tf_op jit(solution)/shard_map/psum | solution.py:12
  6.5 6.8 %copy-start.4 = (s32[2,256]{1,0:T(2,128)S(1)}, s32[2,256]{1,0:T(2,128)}, u32[]{:S(2)}) copy-start(s32[2,256]{1,0:T(2,128)} %param.11) | copy-start | bytes 6148
  13.4 5.6 %slice-start = ((bf16[7,256,7,256]{3,1,2,0:T(8,128)(2,1)}), bf16[1,256,7,256]{3,1,2,0:T(8,128)(2,1)S(1)}, s32[]{:S(2)}) async-start(bf16[7,256,7,256]{3,1,2,0:T(8,128)(2,1)} %param.10), calls=%async_computation.4 | async-start | bytes 1835008 | tf_op jit(solution)/shard_map/slice | solution.py:61
  28.1 231.8 %all-reduce.7.cloned.1.call-start = ((), (), s32[]{:S(2)}) async-start(), calls=%async_computation | async-start | bytes 1835008 | tf_op jit(solution)/shard_map/psum | solution.py:12
  142.9 9.5 %copy-start.2 = (bf16[256,1792]{1,0:T(8,128)(2,1)S(1)}, bf16[256,1792]{1,0:T(8,128)(2,1)}, u32[]{:S(2)}) copy-start(bf16[256,1792]{1,0:T(8,128)(2,1)} %get-tuple-element.56) | copy-start | bytes 2752516
  160.2 230.5 %all-reduce.11.cloned.1.call-start = ((), (), s32[]{:S(2)}) async-start(), calls=%async_computation.2 | async-start | bytes 3670016 | tf_op jit(solution)/shard_map/psum | solution.py:12
  259.9 7.8 %copy-start = (bf16[1792,256]{1,0:T(8,128)(2,1)S(1)}, bf16[1792,256]{1,0:T(8,128)(2,1)}, u32[]{:S(2)}) copy-start(bf16[1792,256]{1,0:T(8,128)(2,1)} %all-reduce.7.cloned.1.call-done) | copy-start | bytes 2752516
  279.4 228.5 %all-reduce.9.cloned.1.call-start = ((), (), s32[]{:S(2)}) async-start(), calls=%async_computation.1 | async-start | bytes 1835008 | tf_op jit(solution)/shard_map/psum | solution.py:12
  390.7 9.7 %copy-start.3 = (bf16[256,1792]{1,0:T(8,128)(2,1)S(1)}, bf16[256,1792]{1,0:T(8,128)(2,1)}, u32[]{:S(2)}) copy-start(bf16[256,1792]{1,0:T(8,128)(2,1)} %get-tuple-element.54) | copy-start | bytes 2752516
  507.9 7.8 %copy-start.1 = (bf16[1792,256]{1,0:T(8,128)(2,1)S(1)}, bf16[1792,256]{1,0:T(8,128)(2,1)}, u32[]{:S(2)}) copy-start(bf16[1792,256]{1,0:T(8,128)(2,1)} %all-reduce.9.cloned.1.call-done) | copy-start | bytes 2752516
Sparse Core Ops, SparseCore 0:
  28.2 114.6 all-reduce.12
  160.3 99.4 all-reduce.6
  279.5 111.1 all-reduce.10
  408.3 99.4 all-reduce.8
where the time goes:
time: 555 us; the launch traced here: 546 us
  waiting for transfers between devices  424 us (76%)
  local copies, waits for them, and re-layouts  65.8 us (12%)
  matrix products  26.3 us (5%)
  other arithmetic  15.8 us (3%)
  between operations  13.6 us (2%)
    psum x4, waiting for transfers between devices, broadcast(): return lax.psum(jnp.where(mine, shard, jnp.zeros_like(shard)), axis)  424 us
    reshape x2, local copies, waits for them, and re-layouts, body(): return current.reshape(row_cycles, block_size, col_cycles, block_size)  20.6 us
    scatter x2, local copies, waits for them, and re-layouts, body(): current = current.at[target].set(old_top, mode='drop')  19.2 us
    dot_general x2, matrix products, body(): jnp.dot(lower_panel, upper_rows, preferred_element_type=jnp.float32)  15.6 us
    unnamed x13, local copies, waits for them, and re-layouts  13 us
    gather x2, local copies, waits for them, and re-layouts, body(): current[jnp.clip(local_at, 0, local_rows - 1)]  11.6 us
  transfers between devices with their start and end apart: 4, of which 4 were waited for; matrix products, arithmetic and copies ran while one was open for 0% of the time, Pallas kernels for 0%

commit v1 on v0

--- a/solution.py
+++ b/solution.py
@@ -9,7 +9,7 @@
 
 def broadcast(shard, axis, root):
     mine = lax.axis_index(axis) == root
-    return lax.psum(jnp.where(mine, shard, jnp.zeros_like(shard)), axis)
+    return jnp.sum(lax.all_gather(jnp.where(mine, shard, jnp.zeros_like(shard)), axis), axis=0)
 
 
 def newton_inverse(diag_block):

time: 555 us -> 763 us (1.37)
  waiting for transfers between devices: 424 us -> 594 us
  other arithmetic: 15.8 us -> 48.1 us
    all_gather x0 -> x4, waiting for transfers between devices: none -> 378 us  [broadcast(): lax.all_gather(jnp.where(mine, shard, jnp.zeros_like(shard)), axis)]
    psum x4 -> x2, waiting for transfers between devices: 424 us -> 216 us  [body(): new_top = lax.psum(picked, 'row').astype(jnp.float32).astype(jnp.bfloat16)]
    reduce_sum x0 -> x4, other arithmetic: none -> 31 us  [broadcast(): jnp.sum(lax.all_gather(jnp.where(mine, shard, jnp.zeros_like(shard)), axi...]
  transfers between devices with their start and end apart: 4 -> 6, of which waited for: 4 -> 6; matrix products, arithmetic and copies ran while one was open for 0% -> 2% of each run, Pallas kernels for 0% -> 0%
where the time goes in v1:
time: 763 us; the launch traced here: 753 us
  waiting for transfers between devices  594 us (78%)
  local copies, waits for them, and re-layouts  65.3 us (9%)
  other arithmetic  48.1 us (6%)
  matrix products  30.9 us (4%)
  between operations  13.9 us (2%)
    all_gather x4, waiting for transfers between devices, broadcast(): lax.all_gather(jnp.where(mine, shard, jnp.zeros_like(shard)), axis)  378 us
    psum x2, waiting for transfers between devices, body(): new_top = lax.psum(picked, 'row').astype(jnp.float32).astype(jnp.bfloat16)  216 us
    reduce_sum x4, other arithmetic, broadcast(): jnp.sum(lax.all_gather(jnp.where(mine, shard, jnp.zeros_like(shard)), axi...  31 us
    reshape x2, local copies, waits for them, and re-layouts, body(): return current.reshape(row_cycles, block_size, col_cycles, block_size)  20.6 us
    scatter x2, local copies, waits for them, and re-layouts, body(): current = current.at[target].set(old_top, mode='drop')  17.9 us
  transfers between devices with their start and end apart: 6, of which 6 were waited for; matrix products, arithmetic and copies ran while one was open for 2% of the time, Pallas kernels for 0%

profile of v1, /device:TPU:32, one launch (start us, length us, event | category | flops | bytes accessed | tf_op | source)
XLA Modules:
  0.0 753.0 jit_solution(10205768175777310580)
XLA Ops:
  6.5 0.7 compare_select_fusion
  7.2 0.8 fusion.98
  8.0 6.8 copy.8
  14.8 5.6 copy.16
  20.5 5.9 gather_fusion
  26.4 1.1 broadcast_select_fusion.1
  27.5 0.6 copy.15
  28.2 1.4 copy.10
  29.9 109.4 %all-reduce.3.cloned.1.call-done = bf16[256,1792]{1,0:T(8,128)(2,1)} async-done(((bf16[256,1792]{1,0:T(8,128)(2,1)}), bf16[256,1792]{1,0:T(8,128)(2,1)}) %all-reduce.3.cloned.1.call-update) | async-done | bytes 917520 | tf_op jit(solution)/shard_map/psum | solution.py:63
  139.4 1.3 convolution_subtract_fusion.5
  140.6 0.4 fusion.17
  141.0 1.3 convolution_subtract_fusion.4
  142.3 0.4 fusion.99
  142.7 1.3 convolution_subtract_fusion.3
  144.0 0.4 fusion.100
  144.4 83.4 %all-gather.8.cloned.1.call-done = bf16[16,256,1792]{2,1,0:T(8,128)(2,1)} async-done(((bf16[1,256,1792]{2,1,0:T(8,128)(2,1)}), bf16[16,256,1792]{2,1,0:T(8,128)(2,1)}) %all-gather.8.cloned.1.call-update) | async-done | bytes 14680080 | tf_op jit(solution)/shard_map/all_gather | solution.py:12
  227.8 7.7 %reduce_sum.48 = bf16[256,1792]{1,0:T(8,128)(2,1)S(1)} reduce(bf16[16,256,1792]{2,1,0:T(8,128)(2,1)} %all-gather.8.cloned.1.call-done, bf16[]{:T(256)} %constant.238.clone.1), dimensions={0}, to_apply=%region_0.1 | reduce | flops 6881280 | bytes 15597570 | tf_op jit(solution)/shard_map/reduce_sum | solution.py:12
  235.6 8.9 %scatter_fusion = bf16[1792,1792]{1,0:T(8,128)(2,1)} fusion(bf16[1792,1792]{1,0:T(8,128)(2,1)} %bitcast.70, s32[256]{0:T(256)S(1)} %bitcast.76, bf16[256,1792]{1,0:T(8,128)(2,1)S(1)} %reduce_sum.48), kind=kCustom, calls=%fused_computation.2 | custom fusion | bytes 2753536 | tf_op jit(solution)/shard_map/scatter | solution.py:66
  244.5 2.3 fusion.9
  246.8 3.0 fusion.3
  249.8 0.3 all-reduce.5.cloned.1.call-start
  250.1 0.6 compare_reduce_fusion
  250.8 105.1 %all-gather.10.cloned.1.call-done = bf16[28672,256]{1,0:T(8,128)(2,1)} async-done(((bf16[1792,256]{1,0:T(8,128)(2,1)}), bf16[28672,256]{1,0:T(8,128)(2,1)}) %all-gather.10.cloned.1.call-update) | async-done | bytes 14680080 | tf_op jit(solution)/shard_map/all_gather | solution.py:12
  355.9 7.8 %reduce_sum.49 = bf16[1792,256]{1,0:T(8,128)(2,1)S(1)} reduce(bf16[16,1792,256]{2,1,0:T(8,128)(2,1)} %bitcast.73, bf16[]{:T(256)} %constant.238.clone.1), dimensions={0}, to_apply=%region_3.4 | reduce | flops 6881280 | bytes 15597570 | tf_op jit(solution)/shard_map/reduce_sum | solution.py:12
  363.7 7.4 subtract_convert_fusion.1
  371.1 3.3 fusion.4
  374.4 5.8 gather_fusion.1
  380.2 1.1 broadcast_select_fusion
  381.4 2.2 slice_select_fusion.1
  383.6 0.4 all-gather.14.cloned.1.call-start
  384.0 106.3 %all-reduce.5.cloned.1.call-done = bf16[256,1792]{1,0:T(8,128)(2,1)} async-done(((bf16[256,1792]{1,0:T(8,128)(2,1)}), bf16[256,1792]{1,0:T(8,128)(2,1)}) %all-reduce.5.cloned.1.call-update) | async-done | bytes 917520 | tf_op jit(solution)/shard_map/psum | solution.py:63
  490.3 1.3 convolution_subtract_fusion.2
  491.6 0.4 fusion.14
  492.0 1.3 convolution_subtract_fusion.1
  493.3 0.4 fusion.101
  493.7 1.3 convolution_subtract_fusion
  495.0 0.4 fusion.102
  495.4 83.3 %all-gather.12.cloned.1.call-done = bf16[4096,1792]{1,0:T(8,128)(2,1)} async-done(((bf16[256,1792]{1,0:T(8,128)(2,1)}), bf16[4096,1792]{1,0:T(8,128)(2,1)}) %all-gather.12.cloned.1.call-update) | async-done | bytes 14680080 | tf_op jit(solution)/shard_map/all_gather | solution.py:12
  578.7 7.7 %reduce_sum.50 = bf16[256,1792]{1,0:T(8,128)(2,1)S(1)} reduce(bf16[16,256,1792]{2,1,0:T(8,128)(2,1)} %bitcast.72, bf16[]{:T(256)} %constant.238.clone.1), dimensions={0}, to_apply=%region_5.6 | reduce | flops 6881280 | bytes 15597570 | tf_op jit(solution)/shard_map/reduce_sum | solution.py:12
  586.4 9.0 %scatter_fusion.1 = bf16[1792,1792]{1,0:T(8,128)(2,1)} fusion(bf16[1792,1792]{1,0:T(8,128)(2,1)} %fusion.4, s32[256]{0:T(256)S(1)} %bitcast.77, bf16[256,1792]{1,0:T(8,128)(2,1)S(1)} %reduce_sum.50), kind=kCustom, calls=%fused_computation.3 | custom fusion | bytes 2753536 | tf_op jit(solution)/shard_map/scatter | solution.py:66
  595.4 2.3 fusion.7
  597.7 3.0 fusion.2
  600.8 106.0 %all-gather.14.cloned.1.call-done = bf16[28672,256]{1,0:T(8,128)(2,1)} async-done(((bf16[1792,256]{1,0:T(8,128)(2,1)}), bf16[28672,256]{1,0:T(8,128)(2,1)}) %all-gather.14.cloned.1.call-update) | async-done | bytes 14680080 | tf_op jit(solution)/shard_map/all_gather | solution.py:12
  706.9 7.8 %reduce_sum.51 = bf16[1792,256]{1,0:T(8,128)(2,1)S(1)} reduce(bf16[16,1792,256]{2,1,0:T(8,128)(2,1)} %bitcast.74, bf16[]{:T(256)} %constant.238.clone.1), dimensions={0}, to_apply=%region_8.9 | reduce | flops 6881280 | bytes 15597570 | tf_op jit(solution)/shard_map/reduce_sum | solution.py:12
  714.7 7.4 subtract_convert_fusion
  722.1 3.3 fusion.5
  725.4 13.0 %reshape.610 = bf16[7,256,7,256]{3,2,1,0:T(8,128)(2,1)} reshape(bf16[1792,1792]{1,0:T(8,128)(2,1)} %fusion.5) | data formatting | bytes 12845056 | tf_op jit(solution)/shard_map/reshape | solution.py:96
  738.4 7.6 %copy.13 = bf16[7,256,7,256]{3,1,2,0:T(8,128)(2,1)} copy(bf16[7,256,7,256]{3,2,1,0:T(8,128)(2,1)} %reshape.610) | data formatting | bytes 12845056 | tf_op jit(solution)/shard_map/reshape | solution.py:96
  (31 shorter events, 0.7 us)
Async XLA Ops:
  6.5 132.8 %all-reduce.3.cloned.1.call-start = ((), (), s32[]{:S(2)}) async-start(), calls=%async_computation.1 | async-start | bytes 1835008 | tf_op jit(solution)/shard_map/psum | solution.py:63
  14.8 5.6 copy-start.2
  20.5 7.1 slice-start
  27.5 200.4 %all-gather.8.cloned.1.call-start = ((), (), s32[]{:S(2)}) async-start(), calls=%async_computation | async-start | bytes 15597568 | tf_op jit(solution)/shard_map/all_gather | solution.py:12
  29.7 326.2 %all-gather.10.cloned.1.call-start = ((), (), s32[]{:S(2)}) async-start(), calls=%async_computation.3 | async-start | bytes 15597568 | tf_op jit(solution)/shard_map/all_gather | solution.py:12
  235.6 8.9 %copy-start = (bf16[256,1792]{1,0:T(8,128)(2,1)S(1)}, bf16[256,1792]{1,0:T(8,128)(2,1)}, u32[]{:S(2)}) copy-start(bf16[256,1792]{1,0:T(8,128)(2,1)} %all-reduce.3.cloned.1.call-done) | copy-start | bytes 2752516
  249.8 240.5 %all-reduce.5.cloned.1.call-start = ((), (), s32[]{:S(2)}) async-start(), calls=%async_computation.2 | async-start | bytes 1835008 | tf_op jit(solution)/shard_map/psum | solution.py:63
  381.3 197.3 %all-gather.12.cloned.1.call-start = ((), (), s32[]{:S(2)}) async-start(), calls=%async_computation.4 | async-start | bytes 15597568 | tf_op jit(solution)/shard_map/all_gather | solution.py:12
  383.6 323.3 %all-gather.14.cloned.1.call-start = ((), (), s32[]{:S(2)}) async-start(), calls=%async_computation.5 | async-start | bytes 15597568 | tf_op jit(solution)/shard_map/all_gather | solution.py:12
  586.4 9.0 %copy-start.1 = (bf16[256,1792]{1,0:T(8,128)(2,1)S(1)}, bf16[256,1792]{1,0:T(8,128)(2,1)}, u32[]{:S(2)}) copy-start(bf16[256,1792]{1,0:T(8,128)(2,1)} %all-reduce.5.cloned.1.call-done) | copy-start | bytes 2752516
Sparse Core Ops, SparseCore 0:
  27.6 111.6 all-reduce.2
  141.2 86.6 all-gather.7
  249.9 105.9 all-gather.9
  381.4 108.8 all-reduce.4
  492.0 86.6 all-gather.11
  600.9 105.9 all-gather.13
